TPU v7x, 512 devices: a whole 4x8x8 slice. The times are simulated.
512 devices in a mesh: rep: 8 (over y), dom: 64 (over x, z, core).
Axes of the slice: x: 4, y: 8, z: 8, core: 2. Of those that a mesh axis runs over, the one named last changes fastest.
Arguments:
- feats: bfloat16 [65536, 256], P(('rep', 'dom')), may hold values from -6 to 6
- w_self: bfloat16 [256, 256], replicated, may hold values from -0.375 to 0.375
- w_neigh: bfloat16 [256, 256], replicated, may hold values from -1.5 to 1.5
- tile_vals: bfloat16 [8, 64, 128, 128, 128], P('rep', 'dom'), may hold values from 0 to 1
- tile_owner: int32 [8, 64, 128], P('rep', 'dom'), may hold values from 0 to 63, as said below
- tile_src: int32 [8, 64, 128], P('rep', 'dom'), may hold values from 0 to 7
- tile_count: int32 [8, 64], P('rep', 'dom'), may hold values from 64 to 128, as said below
- d_out: bfloat16 [65536, 256], P(('rep', 'dom')), may hold values from -6 to 6
Outputs:
- out_feats: bfloat16 [65536, 256], P(('rep', 'dom'))
- d_feats: bfloat16 [65536, 256], P(('rep', 'dom'))
- grad_self: float32 [256, 256], P('dom')
- grad_neigh: float32 [256, 256], P('dom')
Inputs may be any that keep to these rules, and one draw needn't show every extreme that they name: Within one list no two tiles name the same pair of tile_owner and tile_src. Tiles of list (i, j) at positions tile_count[i, j] and beyond are padding.
All inputs are finite; a program needn't handle non-finite values.
Results may differ from a plain program's by a relative error of at most 0.0049.
Values may be sent and summed in bfloat16 or wider, within the bound.
No kernel may reach another device: no remote copies, remote signals or barrier semaphores. Data moves between devices by JAX's collectives and lax.ppermute only.
A program may use at most 128 MiB of HBM per device.

v0:
```python
import jax
import jax.numpy as jnp
from jax import lax
from jax.experimental import pallas as pl
from jax.experimental.pallas import tpu as pltpu
from jax.sharding import Mesh
from jax.sharding import PartitionSpec as P


BF = jnp.bfloat16
F32 = jnp.float32
NX, NZ, NC, NR = 4, 8, 2, 8
T = 128
H = 256
TILES = 128
SLOTS = 144
HALF = NX * NZ
DEG = 8
GRAD = 8
BLK = H + 2 * DEG
VMEM = pl.BlockSpec(memory_space=pltpu.VMEM)
SMEM = pl.BlockSpec(memory_space=pltpu.SMEM)
HBM = pl.BlockSpec(memory_space=pltpu.HBM)
PARAMS = pltpu.CompilerParams(vmem_limit_bytes=20 * 1024 * 1024)
NT = (((1,), (1,)), ((), ()))
TN = (((0,), (0,)), ((), ()))


def dot(a, b, dims=(((1,), (0,)), ((), ()))):
    return lax.dot_general(a, b, dims, preferred_element_type=F32)


def call(kernel, out_shape, *args, scratch=(), cost=None):
    def spec(a):
        return SMEM if a.dtype == jnp.int32 else HBM if a.shape == (TILES, T, T) else VMEM

    def place(a):
        s = spec(a)
        return a if s is SMEM else pltpu.with_memory_space_constraint(a, s.memory_space)

    args = [place(a) for a in args]
    return pl.pallas_call(
        kernel,
        in_specs=[spec(a) for a in args],
        out_specs=jax.tree.map(spec, out_shape, is_leaf=lambda a: hasattr(a, "dtype")),
        out_shape=out_shape,
        scratch_shapes=scratch,
        compiler_params=PARAMS,
        cost_estimate=cost,
    )(*args)


def split_degree(deg):
    high = deg.astype(BF).astype(F32)
    return jnp.concatenate([high, deg - high], axis=0).astype(BF)


def add_blocks(blocks):
    sums, deg = 0.0, 0.0
    for block in blocks:
        block = block.astype(F32)
        sums = sums + block[:H]
        deg = deg + block[H : H + DEG]
        if block.shape[0] == BLK:
            deg = deg + block[H + DEG :]
    return sums, deg


def spread_kernel(feats, out):
    block = feats[...].astype(F32).T.astype(BF)
    for r in range(NR):
        out[r] = block


def spread(feats):
    return call(spread_kernel, pltpu.VMEM((NR, H, T), BF), feats)


def order_kernel(owners, sources, meta, ids, owner_slots, srcs, pairs, seen):
    count, my_core = meta[0], meta[2]

    def bucket(t):
        return ((owners[t] & 1) ^ my_core) * NR + sources[t]

    @pl.loop(0, NC * NR)
    def _(b):
        seen[b] = 0

    @pl.loop(0, count)
    def _(t):
        seen[bucket(t)] = seen[bucket(t)] + 1

    for far in range(NC):
        at = jnp.int32(far * SLOTS)
        for src in range(NR):
            size = seen[far * NR + src]
            seen[far * NR + src] = at
            at = at + size

            @pl.when(size % 2 == 1)
            def _():
                ids[at], owner_slots[at], srcs[at] = -1, 0, src

            at = at + size % 2
        pairs[far] = (at - far * SLOTS) // 2

    @pl.loop(0, count)
    def _(t):
        at = seen[bucket(t)]
        seen[bucket(t)] = at + 1
        ids[at] = t
        owner_slots[at] = owners[t] >> 1
        srcs[at] = sources[t]


def order(owners, sources, meta):
    lists = jax.ShapeDtypeStruct((NC * SLOTS,), jnp.int32)
    out_shape = (lists, lists, lists, jax.ShapeDtypeStruct((NC,), jnp.int32))
    scratch = [pltpu.SMEM((NC * NR,), jnp.int32)]
    return call(order_kernel, out_shape, owners, sources, meta, scratch=scratch)


def over_pairs(far, ids, pairs, vals, buffers, prepare, step):
    tiles, sems = buffers
    first, n_pairs = far * SLOTS, pairs[far]

    def copy(k):
        return pltpu.make_async_copy(vals.at[ids[first + k]], tiles.at[k], sems.at[k])

    @pl.loop(0, n_pairs * 2)
    def _(k):
        real = ids[first + k] >= 0

        @pl.when(real)
        def _():
            copy(k).start()

        @pl.when(jnp.logical_not(real))
        def _():
            tiles[k] = jnp.zeros((T, T), BF)

    prepare()

    def run(ps):
        for p in ps:
            copy(p * 2).wait()

            @pl.when(ids[first + p * 2 + 1] >= 0)
            def _():
                copy(p * 2 + 1).wait()

        step([(first + p * 2, tiles[pl.ds(p * 2, 2)].reshape(2 * T, T)) for p in ps])

    @pl.loop(0, n_pairs // 2)
    def _(q):
        run([q * 2, q * 2 + 1])

    @pl.when(n_pairs % 2 == 1)
    def _():
        run([n_pairs - 1])


def forward_sums(far, ids, slots, srcs, pairs, my_x, vals, panel, acc, lhs, buffers):
    def prepare():
        acc[...] = jnp.zeros(acc.shape, F32)
        for s in range(NR):
            lhs[s, :H] = panel[s]
            lhs[s, H:] = jnp.ones((2 * DEG, T), BF)

    def step(tiles):
        prods = [dot(lhs[srcs[n]], pair, NT) for n, pair in tiles]
        for (n, _), prod in zip(tiles, prods):
            for k in range(2):
                slot = (slots[n + k] - my_x[0] * NZ) & (HALF - 1)
                acc[slot] = acc[slot] + prod[: H + DEG, k * T : (k + 1) * T]

    over_pairs(far, ids, pairs, vals, buffers, prepare, step)


def forward_far_kernel(ids, slots, srcs, pairs, my_x, vals, panel, out, acc, lhs, *buffers):
    forward_sums(1, ids, slots, srcs, pairs, my_x, vals, panel, acc, lhs, buffers)

    @pl.loop(0, HALF)
    def _(b):
        out[b, :H] = acc[b, :H].astype(BF)
        out[b, H:] = split_degree(acc[b, H:])


def forward_near_kernel(ids, slots, srcs, pairs, my_x, vals, panel, out, lhs, *buffers):
    forward_sums(0, ids, slots, srcs, pairs, my_x, vals, panel, out, lhs, buffers)


FORWARD_COST = pl.CostEstimate(flops=64 * 2 * BLK * T * T, bytes_accessed=2**21, transcendentals=0)
BACKWARD_COST = FORWARD_COST
BUFFERS = [pltpu.VMEM((SLOTS, T, T), BF), pltpu.SemaphoreType.DMA((SLOTS,))]


def forward_far(lists, my_x, tiles, panel):
    scratch = [pltpu.VMEM((HALF, H + DEG, T), F32), pltpu.VMEM((NR, BLK, T), BF), *BUFFERS]
    out_shape = pltpu.VMEM((HALF, BLK, T), BF)
    return call(forward_far_kernel, out_shape, *lists, my_x, tiles, panel, scratch=scratch, cost=FORWARD_COST)


def forward_near(lists, my_x, tiles, panel):
    scratch = [pltpu.VMEM((NR, BLK, T), BF), *BUFFERS]
    out_shape = pltpu.VMEM((HALF, H + DEG, T), F32)
    return call(forward_near_kernel, out_shape, *lists, my_x, tiles, panel, scratch=scratch, cost=FORWARD_COST)


def core_sum(near, other, dx):
    def kernel(a, b, out):
        @pl.loop(0, NZ)
        def _(z):
            sums, deg = add_blocks([a[dx * NZ + z], b[dx * NZ + z]])
            out[z, :H] = sums.astype(BF)
            out[z, H:] = split_degree(deg)

    return call(kernel, pltpu.VMEM((NZ, BLK, T), BF), near, other)


def x_sum_kernel(near, other, *refs):
    *parts, out = refs

    @pl.loop(0, NZ)
    def _(z):
        sums, deg = add_blocks([p[z] for p in (near, other, *parts)])
        out[z, :H] = sums.astype(BF)
        out[z, H:] = split_degree(deg)


def x_sum(near, other, parts):
    return call(x_sum_kernel, pltpu.VMEM((NZ, BLK, T), BF), near, other, *parts)


def node_kernel(parts, feats, d_out, w_self, w_neigh, out_feats, d_sum, base, grads, pairs):
    sums, deg = add_blocks([parts[z] for z in range(NZ)])
    deg = 1.0 + deg[:1]
    mean_t = (sums / deg).astype(BF)
    pre = dot(feats[...], w_self[...]) + dot(mean_t, w_neigh[...], TN)
    gate = jax.nn.sigmoid(pre)
    out_feats[...] = (pre * gate).astype(BF)
    d_pre = (d_out[...].astype(F32) * gate * (1.0 + pre * (1.0 - gate))).astype(BF)
    d_sum_t = (dot(w_neigh[...], d_pre, NT) / deg).astype(BF)
    for z in range(NZ):
        d_sum[z] = d_sum_t
    base[...] = dot(w_self[...], d_pre, NT)
    rows = GRAD // 2
    for part, grad in enumerate((dot(feats[...], d_pre, TN), dot(mean_t, d_pre))):
        for g in range(H // rows):
            pairs[g, part * rows : (part + 1) * rows] = grad[g * rows : (g + 1) * rows]
    grads[...] = pairs[...].astype(BF)


def node(parts, feats, d_out, w_self, w_neigh):
    out_shape = (
        jax.ShapeDtypeStruct((T, H), BF),
        pltpu.VMEM((NZ, H, T), BF),
        pltpu.VMEM((H, T), F32),
        pltpu.VMEM((NX * NZ * NC, GRAD, H), BF),
    )
    scratch = [pltpu.VMEM((NX * NZ * NC, GRAD, H), F32)]
    return call(node_kernel, out_shape, parts, feats, d_out, w_self, w_neigh, scratch=scratch)


def backward_sums(far, ids, slots, srcs, pairs, my_x, vals, pieces, start, acc, lhs, buffers):
    def prepare():
        acc[...] = start()
        for k in range(NX):
            lhs[k * NZ : (k + 1) * NZ] = pieces[k][...]

    def block(n):
        back = my_x[0] - (slots[n] >> 3)
        return lhs[(back & (NX - 1)) * NZ + (slots[n] & (NZ - 1))]

    def step(tiles):
        sides = [jnp.concatenate([block(n), block(n + 1)], axis=1) for n, _ in tiles]
        prods = [dot(side, pair) for side, (_, pair) in zip(sides, tiles)]
        for (n, _), prod in zip(tiles, prods):
            acc[srcs[n]] = acc[srcs[n]] + prod

    over_pairs(far, ids, pairs, vals, buffers, prepare, step)


def backward_near_kernel(ids, slots, srcs, pairs, my_x, vals, *refs):
    *pieces, out, lhs, tiles, sems = refs
    zeros = lambda: jnp.zeros(out.shape, F32)
    backward_sums(0, ids, slots, srcs, pairs, my_x, vals, pieces, zeros, out, lhs, (tiles, sems))


def backward_far_kernel(ids, slots, srcs, pairs, my_x, vals, *refs):
    *pieces, near, grads, out, acc, lhs, tiles, sems = refs
    start = lambda: near[...]
    backward_sums(1, ids, slots, srcs, pairs, my_x, vals, pieces, start, acc, lhs, (tiles, sems))
    grad = jnp.sum(grads[...].astype(F32), axis=0)
    high = grad.astype(BF).astype(F32)
    parts = [p[:, k : k + T] for p in (high, grad - high) for k in range(0, H, T)]
    grad_rows = jnp.concatenate(parts, axis=0).astype(BF)
    for s in range(NR):
        out[s, :H] = acc[s].astype(BF)
        out[s, H:] = grad_rows


def backward_near(lists, my_x, tiles, pieces):
    scratch = [pltpu.VMEM((HALF, H, T), BF), *BUFFERS]
    out_shape = pltpu.VMEM((NR, H, T), F32)
    args = (*lists, my_x, tiles, *pieces)
    return call(backward_near_kernel, out_shape, *args, scratch=scratch, cost=BACKWARD_COST)


def backward_far(lists, my_x, tiles, pieces, near, grads):
    scratch = [pltpu.VMEM((NR, H, T), F32), pltpu.VMEM((HALF, H, T), BF), *BUFFERS]
    out_shape = pltpu.VMEM((NR, H + 4 * GRAD, T), BF)
    args = (*lists, my_x, tiles, *pieces, near, grads)
    return call(backward_far_kernel, out_shape, *args, scratch=scratch, cost=BACKWARD_COST)


def final_kernel(parts, base, out, *grads):
    total = parts[0].astype(F32)
    for r in range(1, NR):
        total = total + parts[r].astype(F32)
    out[...] = (base[...] + total[:H]).T.astype(BF)
    rows = GRAD // 2
    for k in range(H // T):
        high, low = (total[H + (2 * p + k) * GRAD :][:GRAD] for p in range(2))
        for part, grad in enumerate(grads):
            grad[:, k * T : (k + 1) * T] = (high + low)[part * rows : (part + 1) * rows]


def final(parts, base):
    grad = jax.ShapeDtypeStruct((GRAD // 2, H), F32)
    return call(final_kernel, (jax.ShapeDtypeStruct((T, H), BF), grad, grad), parts, base)


def shift(size, by):
    return [(i, (i + by) % size) for i in range(size)]


def layer(feats, w_self, w_neigh, tile_vals, tile_owner, tile_src, tile_count, d_out):
    tiles = tile_vals[0, 0]
    my_x = lax.axis_index("x").reshape(1)
    meta = jnp.stack([tile_count[0, 0], lax.axis_index("x"), lax.axis_index("core")])
    swap = shift(NC, 1)

    panel = lax.all_to_all(spread(feats), "rep", 0, 0)
    lists = order(tile_owner[0, 0], tile_src[0, 0], meta)
    far = forward_far(lists, my_x, tiles, panel)
    near = forward_near(lists, my_x, tiles, panel)
    other = lax.ppermute(far, "core", swap)
    parts = [lax.ppermute(core_sum(near, other, k), "x", shift(NX, k)) for k in range(1, NX)]
    mine = lax.all_to_all(x_sum(near, other, parts), "z", 0, 0)

    out_feats, d_sum, base, grads = node(mine, feats, d_out, w_self, w_neigh)

    def shifted(k):
        return lax.ppermute(column, "x", shift(NX, k))

    def swapped(k):
        return lax.ppermute(pieces[k], "core", swap)

    grads = lax.all_to_all(grads, ("x", "z", "core"), 0, 0)
    column = lax.all_to_all(d_sum, "z", 0, 0)
    pieces = [column] + [shifted(k) for k in range(1, NX)]
    others = [swapped(k) for k in range(NX)]
    back = backward_near(lists, my_x, tiles, pieces)
    back = backward_far(lists, my_x, tiles, others, back, grads)
    return (out_feats, *final(lax.all_to_all(back, "rep", 0, 0), base))


def solution(mesh):
    split = Mesh(mesh.devices.reshape(NR, NX, NZ, NC), ("rep", "x", "z", "core"))
    dom = ("x", "z", "core")
    nodes = P(("rep", *dom), None)
    in_specs = (
        nodes,
        P(),
        P(),
        P("rep", dom, None, None, None),
        P("rep", dom, None),
        P("rep", dom, None),
        P("rep", dom),
        nodes,
    )
    out_specs = (nodes, nodes, P(dom, None), P(dom, None))
    return jax.shard_map(layer, mesh=split, in_specs=in_specs, out_specs=out_specs, check_vma=False)
```

profile of v0, /device:TPU:1, one launch (start us, length us, event | category | flops | bytes accessed | tf_op | source)
XLA Modules:
  0.0 207.8 jit_solution(4793744903418311385)
XLA Ops:
  0.6 0.0 copy-start
  0.6 0.8 copy-done
  1.5 0.9 shard_map.112
  2.4 7.6 %all-to-all-start = ((bf16[8,256,128]{2,1,0:T(8,128)(2,1)}), bf16[8,256,128]{2,1,0:T(8,128)(2,1)S(1)}, u32[]{:S(2)}, u32[]{:S(2)}) async-start(bf16[8,256,128]{2,1,0:T(8,128)(2,1)} %shard_map.112), calls=%async_computation | async-start | bytes 1048576 | tf_op jit(solution)/shard_map/all_to_all | solution.py:344
  10.7 0.1 pad_add_fusion.meta
  10.8 0.0 copy-start.5
  10.8 0.7 copy-done.5
  11.4 0.0 copy-start.6
  11.4 0.7 copy-done.6
  12.1 4.1 %shard_map.111 = (s32[288]{0:T(512)S(1)}, s32[288]{0:T(512)S(1)}, s32[288]{0:T(512)S(1)}, s32[2]{0:T(128)S(1)}) custom-call(s32[128]{0:T(128)S(1)} %bitcast.7, s32[128]{0:T(128)S(1)} %bitcast.8, s32[3]{0:T(128)S(1)} %pad_add_fusion.meta), custom_call_target="tpu_custom_call" | custom-call | tf_op jit(solution)/shard_map/pallas_call | solution.py:42
  16.2 8.8 %all-to-all-done.panel = bf16[8,256,128]{2,1,0:T(8,128)(2,1)S(1)} async-done(((bf16[8,256,128]{2,1,0:T(8,128)(2,1)}), bf16[8,256,128]{2,1,0:T(8,128)(2,1)S(1)}, u32[]{:S(2)}, u32[]{:S(2)}) %all-to-all-start) | async-done | bytes 524320 | tf_op jit(solution)/shard_map/all_to_all | solution.py:344
  25.0 7.4 %shard_map.114 = bf16[32,272,128]{2,1,0:T(8,128)(2,1)S(1)} custom-call(s32[288]{0:T(512)S(1)} %get-tuple-element.15.ids, s32[288]{0:T(512)S(1)} %get-tuple-element.16.slots, s32[288]{0:T(512)S(1)} %get-tuple-element.17.srcs, s32[2]{0:T(128)S(1)} %get-tuple-element.18.pairs, s32[1]{0:T(128)} %bitcast.3.my_x, bf16[128,128,128]{2,1,0:T(8,128)(2,1)} %bitcast.9, ...), custom_call_target="tpu_custom_call" | custom-call | flops 570425344 | bytes 2097152 | tf_op jit(solution)/shard_map/pallas_call | solution.py:42
  32.4 4.8 %collective-permute-start = (bf16[32,272,128]{2,1,0:T(8,128)(2,1)S(1)}, bf16[32,272,128]{2,1,0:T(8,128)(2,1)S(1)}, u32[]{:S(2)}, u32[]{:S(2)}) collective-permute-start(bf16[32,272,128]{2,1,0:T(8,128)(2,1)S(1)} %shard_map.114), channel_id=1, source_target_pairs={{0,1},{1,0},{2,3},{3,2},{4,5},{5,4},{6,7},{7,6},{8,9},{9,8},{10,11... | collective-permute-start | bytes 6684680 | tf_op jit(solution)/shard_map/ppermute | solution.py:348
  37.2 7.6 %shard_map.113.a.near = f32[32,264,128]{2,1,0:T(8,128)S(1)} custom-call(s32[288]{0:T(512)S(1)} %get-tuple-element.15.ids, s32[288]{0:T(512)S(1)} %get-tuple-element.16.slots, s32[288]{0:T(512)S(1)} %get-tuple-element.17.srcs, s32[2]{0:T(128)S(1)} %get-tuple-element.18.pairs, s32[1]{0:T(128)} %bitcast.3.my_x, bf16[128,128,128]{2,1,0:T(8,128)(2,1)} %bitcast.10, ...), custom_call_target="tpu_custom_call" | custom-call | flops 570425344 | bytes 2097152 | tf_op jit(solution)/shard_map/pallas_call | solution.py:42
  44.8 0.0 collective-permute-done.b.other
  44.9 0.2 shard_map.115
  45.0 2.9 %collective-permute-start.1 = (bf16[8,272,128]{2,1,0:T(8,128)(2,1)S(1)}, bf16[8,272,128]{2,1,0:T(8,128)(2,1)S(1)}, u32[]{:S(2)}, u32[]{:S(2)}) collective-permute-start(bf16[8,272,128]{2,1,0:T(8,128)(2,1)S(1)} %shard_map.115), channel_id=1, source_target_pairs={{0,16},{16,32},{32,48},{48,0},{1,17},{17,33},{33,49},{49,1},{2,18}... | collective-permute-start | bytes 1671176 | tf_op jit(solution)/shard_map/ppermute | solution.py:349
  48.0 0.2 shard_map.116
  48.2 4.6 %collective-permute-start.2 = (bf16[8,272,128]{2,1,0:T(8,128)(2,1)S(1)}, bf16[8,272,128]{2,1,0:T(8,128)(2,1)S(1)}, u32[]{:S(2)}, u32[]{:S(2)}) collective-permute-start(bf16[8,272,128]{2,1,0:T(8,128)(2,1)S(1)} %shard_map.116), channel_id=1, source_target_pairs={{0,32},{16,48},{32,0},{48,16},{1,33},{17,49},{33,1},{49,17},{2,34}... | collective-permute-start | bytes 1671176 | tf_op jit(solution)/shard_map/ppermute | solution.py:349
  52.7 0.2 shard_map.117
  52.9 0.0 copy-start.1
  52.9 0.0 copy-start.2
  52.9 0.0 copy-start.3
  52.9 0.0 copy-start.4
  53.0 4.1 %collective-permute-start.3 = (bf16[8,272,128]{2,1,0:T(8,128)(2,1)S(1)}, bf16[8,272,128]{2,1,0:T(8,128)(2,1)S(1)}, u32[]{:S(2)}, u32[]{:S(2)}) collective-permute-start(bf16[8,272,128]{2,1,0:T(8,128)(2,1)S(1)} %shard_map.117), channel_id=1, source_target_pairs={{0,48},{16,0},{32,16},{48,32},{1,49},{17,1},{33,17},{49,33},{2,50}... | collective-permute-start | bytes 1671176 | tf_op jit(solution)/shard_map/ppermute | solution.py:349
  57.1 4.6 %collective-permute-done.1.refs_0_ = bf16[8,272,128]{2,1,0:T(8,128)(2,1)S(1)} collective-permute-done((bf16[8,272,128]{2,1,0:T(8,128)(2,1)S(1)}, bf16[8,272,128]{2,1,0:T(8,128)(2,1)S(1)}, u32[]{:S(2)}, u32[]{:S(2)}) %collective-permute-start.1) | collective-permute-done | bytes 557088 | tf_op jit(solution)/shard_map/ppermute | solution.py:349
  61.7 12.5 %collective-permute-done.2.refs_1_ = bf16[8,272,128]{2,1,0:T(8,128)(2,1)S(1)} collective-permute-done((bf16[8,272,128]{2,1,0:T(8,128)(2,1)S(1)}, bf16[8,272,128]{2,1,0:T(8,128)(2,1)S(1)}, u32[]{:S(2)}, u32[]{:S(2)}) %collective-permute-start.2) | collective-permute-done | bytes 557088 | tf_op jit(solution)/shard_map/ppermute | solution.py:349
  74.1 2.2 %collective-permute-done.3.refs_2_ = bf16[8,272,128]{2,1,0:T(8,128)(2,1)S(1)} collective-permute-done((bf16[8,272,128]{2,1,0:T(8,128)(2,1)S(1)}, bf16[8,272,128]{2,1,0:T(8,128)(2,1)S(1)}, u32[]{:S(2)}, u32[]{:S(2)}) %collective-permute-start.3) | collective-permute-done | bytes 557088 | tf_op jit(solution)/shard_map/ppermute | solution.py:349
  76.4 0.4 shard_map.118
  76.8 27.8 %all_to_all.25.parts = bf16[8,272,128]{2,1,0:T(8,128)(2,1)S(1)} all-to-all(bf16[8,272,128]{2,1,0:T(8,128)(2,1)S(1)} %shard_map.118), channel_id=1, replica_groups=mesh['rep'=8,'x'=4,'z'=8,'core'=2] {'z'}, dimensions={0} | all-to-all | bytes 1114112 | tf_op jit(solution)/shard_map/all_to_all | solution.py:350
  104.6 0.0 copy-done.1
  104.6 0.0 copy-done.2
  104.6 0.0 copy-done.3
  104.6 0.0 copy-done.4
  104.6 1.3 shard_map.119
  106.0 17.8 %all_to_all.26.refs_0_ = bf16[8,256,128]{2,1,0:T(8,128)(2,1)S(1)} all-to-all(bf16[8,256,128]{2,1,0:T(8,128)(2,1)S(1)} %get-tuple-element.20), channel_id=1, replica_groups=mesh['rep'=8,'x'=4,'z'=8,'core'=2] {'z'}, dimensions={0} | all-to-all | bytes 1048576 | tf_op jit(solution)/shard_map/all_to_all | solution.py:361
  123.8 5.7 %collective-permute-start.9 = (bf16[8,256,128]{2,1,0:T(8,128)(2,1)S(1)}, bf16[8,256,128]{2,1,0:T(8,128)(2,1)}, u32[]{:S(2)}, u32[]{:S(2)}) collective-permute-start(bf16[8,256,128]{2,1,0:T(8,128)(2,1)S(1)} %all_to_all.26.refs_0_), channel_id=1, source_target_pairs={{0,48},{16,0},{32,16},{48,32},{1,49},{17,1},{33,17},{49,33},{2,50}... | collective-permute-start | bytes 1572872 | tf_op jit(solution)/shard_map/ppermute | solution.py:355
  129.5 2.8 %collective-permute-start.7 = (bf16[8,256,128]{2,1,0:T(8,128)(2,1)S(1)}, bf16[8,256,128]{2,1,0:T(8,128)(2,1)}, u32[]{:S(2)}, u32[]{:S(2)}) collective-permute-start(bf16[8,256,128]{2,1,0:T(8,128)(2,1)S(1)} %all_to_all.26.refs_0_), channel_id=1, source_target_pairs={{0,32},{16,48},{32,0},{48,16},{1,33},{17,49},{33,1},{49,17},{2,34}... | collective-permute-start | bytes 1572872 | tf_op jit(solution)/shard_map/ppermute | solution.py:355
  132.3 1.9 collective-permute-start.5
  134.3 5.6 %collective-permute-start.4 = (bf16[8,256,128]{2,1,0:T(8,128)(2,1)S(1)}, bf16[8,256,128]{2,1,0:T(8,128)(2,1)S(1)}, u32[]{:S(2)}, u32[]{:S(2)}) collective-permute-start(bf16[8,256,128]{2,1,0:T(8,128)(2,1)S(1)} %all_to_all.26.refs_0_), channel_id=1, source_target_pairs={{0,1},{1,0},{2,3},{3,2},{4,5},{5,4},{6,7},{7,6},{8,9},{9,8},{10,11... | collective-permute-start | bytes 1572872 | tf_op jit(solution)/shard_map/ppermute | solution.py:358
  139.8 0.0 collective-permute-done.9.refs_3_
  139.9 15.0 %collective-permute-start.10 = (bf16[8,256,128]{2,1,0:T(8,128)(2,1)}, bf16[8,256,128]{2,1,0:T(8,128)(2,1)S(1)}, u32[]{:S(2)}, u32[]{:S(2)}) collective-permute-start(bf16[8,256,128]{2,1,0:T(8,128)(2,1)} %collective-permute-done.9.refs_3_), channel_id=1, source_target_pairs={{0,1},{1,0},{2,3},{3,2},{4,5},{5,4},{6,7},{7,6},{8,9},{9,8},{10,11... | collective-permute-start | bytes 1572872 | tf_op jit(solution)/shard_map/ppermute | solution.py:358
  154.8 0.0 collective-permute-done.7.refs_2_
  154.8 1.9 collective-permute-start.8
  156.8 1.4 collective-permute-done.5.refs_1_
  158.1 2.4 %collective-permute-start.6 = (bf16[8,256,128]{2,1,0:T(8,128)(2,1)}, bf16[8,256,128]{2,1,0:T(8,128)(2,1)}, u32[]{:S(2)}, u32[]{:S(2)}) collective-permute-start(bf16[8,256,128]{2,1,0:T(8,128)(2,1)} %collective-permute-done.5.refs_1_), channel_id=1, source_target_pairs={{0,1},{1,0},{2,3},{3,2},{4,5},{5,4},{6,7},{7,6},{8,9},{9,8},{10,11... | collective-permute-start | bytes 1572872 | tf_op jit(solution)/shard_map/ppermute | solution.py:358
  160.5 6.0 %all-to-all-start.3 = ((bf16[64,8,256]{2,1,0:T(8,128)(2,1)}), bf16[64,8,256]{2,1,0:T(8,128)(2,1)S(1)}, u32[]{:S(2)}, u32[]{:S(2)}) async-start(bf16[64,8,256]{2,1,0:T(8,128)(2,1)} %get-tuple-element.21), calls=%async_computation.3 | async-start | bytes 524288 | tf_op jit(solution)/shard_map/all_to_all | solution.py:360
  166.5 7.5 %shard_map.120.refs_4_ = f32[8,256,128]{2,1,0:T(8,128)S(1)} custom-call(s32[288]{0:T(512)S(1)} %get-tuple-element.15.ids, s32[288]{0:T(512)S(1)} %get-tuple-element.16.slots, s32[288]{0:T(512)S(1)} %get-tuple-element.17.srcs, s32[2]{0:T(128)S(1)} %get-tuple-element.18.pairs, s32[1]{0:T(128)} %bitcast.3.my_x, bf16[128,128,128]{2,1,0:T(8,128)(2,1)} %bitcast.11, ...), custom_call_target="tpu_custom_call" | custom-call | flops 570425344 | bytes 2097152 | tf_op jit(solution)/shard_map/pallas_call | solution.py:42
  174.1 4.4 %all-to-all-done.3.refs_5_ = bf16[64,8,256]{2,1,0:T(8,128)(2,1)S(1)} async-done(((bf16[64,8,256]{2,1,0:T(8,128)(2,1)}), bf16[64,8,256]{2,1,0:T(8,128)(2,1)S(1)}, u32[]{:S(2)}, u32[]{:S(2)}) %all-to-all-start.3) | async-done | bytes 262176 | tf_op jit(solution)/shard_map/all_to_all | solution.py:360
  178.5 0.0 collective-permute-done.4.refs_0_
  178.5 0.0 collective-permute-done.10.refs_3_
  178.5 0.0 collective-permute-done.8.refs_2_
  178.5 0.0 collective-permute-done.6.refs_1_
  178.5 6.8 %shard_map.121 = bf16[8,288,128]{2,1,0:T(8,128)(2,1)S(1)} custom-call(s32[288]{0:T(512)S(1)} %get-tuple-element.15.ids, s32[288]{0:T(512)S(1)} %get-tuple-element.16.slots, s32[288]{0:T(512)S(1)} %get-tuple-element.17.srcs, s32[2]{0:T(128)S(1)} %get-tuple-element.18.pairs, s32[1]{0:T(128)} %bitcast.3.my_x, bf16[128,128,128]{2,1,0:T(8,128)(2,1)} %bitcast.12, ...), custom_call_target="tpu_custom_call" | custom-call | flops 570425344 | bytes 2097152 | tf_op jit(solution)/shard_map/pallas_call | solution.py:42
  185.3 21.8 %all_to_all.27.parts = bf16[8,288,128]{2,1,0:T(8,128)(2,1)S(1)} all-to-all(bf16[8,288,128]{2,1,0:T(8,128)(2,1)S(1)} %shard_map.121), channel_id=1, replica_groups=mesh['rep'=8,'x'=4,'z'=8,'core'=2] {'rep'}, dimensions={0} | all-to-all | bytes 1179648 | tf_op jit(solution)/shard_map/all_to_all | solution.py:366
  207.0 0.8 shard_map.122
Async XLA Ops:
  0.6 0.8 copy-start
  2.4 22.6 %all-to-all-start = ((bf16[8,256,128]{2,1,0:T(8,128)(2,1)}), bf16[8,256,128]{2,1,0:T(8,128)(2,1)S(1)}, u32[]{:S(2)}, u32[]{:S(2)}) async-start(bf16[8,256,128]{2,1,0:T(8,128)(2,1)} %shard_map.112), calls=%async_computation | async-start | bytes 1048576 | tf_op jit(solution)/shard_map/all_to_all | solution.py:344
  10.8 0.7 copy-start.5
  11.4 0.7 copy-start.6
  32.4 12.5 %collective-permute-start = (bf16[32,272,128]{2,1,0:T(8,128)(2,1)S(1)}, bf16[32,272,128]{2,1,0:T(8,128)(2,1)S(1)}, u32[]{:S(2)}, u32[]{:S(2)}) collective-permute-start(bf16[32,272,128]{2,1,0:T(8,128)(2,1)S(1)} %shard_map.114), channel_id=1, source_target_pairs={{0,1},{1,0},{2,3},{3,2},{4,5},{5,4},{6,7},{7,6},{8,9},{9,8},{10,11... | collective-permute-start | bytes 6684680 | tf_op jit(solution)/shard_map/ppermute | solution.py:348
  45.0 16.6 %collective-permute-start.1 = (bf16[8,272,128]{2,1,0:T(8,128)(2,1)S(1)}, bf16[8,272,128]{2,1,0:T(8,128)(2,1)S(1)}, u32[]{:S(2)}, u32[]{:S(2)}) collective-permute-start(bf16[8,272,128]{2,1,0:T(8,128)(2,1)S(1)} %shard_map.115), channel_id=1, source_target_pairs={{0,16},{16,32},{32,48},{48,0},{1,17},{17,33},{33,49},{49,1},{2,18}... | collective-permute-start | bytes 1671176 | tf_op jit(solution)/shard_map/ppermute | solution.py:349
  48.2 26.0 %collective-permute-start.2 = (bf16[8,272,128]{2,1,0:T(8,128)(2,1)S(1)}, bf16[8,272,128]{2,1,0:T(8,128)(2,1)S(1)}, u32[]{:S(2)}, u32[]{:S(2)}) collective-permute-start(bf16[8,272,128]{2,1,0:T(8,128)(2,1)S(1)} %shard_map.116), channel_id=1, source_target_pairs={{0,32},{16,48},{32,0},{48,16},{1,33},{17,49},{33,1},{49,17},{2,34}... | collective-permute-start | bytes 1671176 | tf_op jit(solution)/shard_map/ppermute | solution.py:349
  52.9 51.7 %copy-start.1 = (bf16[128,256]{1,0:T(8,128)(2,1)S(1)}, bf16[128,256]{1,0:T(8,128)(2,1)}, u32[]{:S(2)}) copy-start(bf16[128,256]{1,0:T(8,128)(2,1)} %feats.3) | copy-start | bytes 196612
  52.9 51.7 %copy-start.2 = (bf16[256,256]{1,0:T(8,128)(2,1)S(1)}, bf16[256,256]{1,0:T(8,128)(2,1)}, u32[]{:S(2)}) copy-start(bf16[256,256]{1,0:T(8,128)(2,1)} %w_self.1) | copy-start | bytes 393220
  52.9 51.7 %copy-start.3 = (bf16[256,256]{1,0:T(8,128)(2,1)S(1)}, bf16[256,256]{1,0:T(8,128)(2,1)}, u32[]{:S(2)}) copy-start(bf16[256,256]{1,0:T(8,128)(2,1)} %w_neigh.1) | copy-start | bytes 393220
  52.9 51.7 %copy-start.4 = (bf16[128,256]{1,0:T(8,128)(2,1)S(1)}, bf16[128,256]{1,0:T(8,128)(2,1)}, u32[]{:S(2)}) copy-start(bf16[128,256]{1,0:T(8,128)(2,1)} %d_out.1) | copy-start | bytes 196612
  53.0 23.4 %collective-permute-start.3 = (bf16[8,272,128]{2,1,0:T(8,128)(2,1)S(1)}, bf16[8,272,128]{2,1,0:T(8,128)(2,1)S(1)}, u32[]{:S(2)}, u32[]{:S(2)}) collective-permute-start(bf16[8,272,128]{2,1,0:T(8,128)(2,1)S(1)} %shard_map.117), channel_id=1, source_target_pairs={{0,48},{16,0},{32,16},{48,32},{1,49},{17,1},{33,17},{49,33},{2,50}... | collective-permute-start | bytes 1671176 | tf_op jit(solution)/shard_map/ppermute | solution.py:349
  123.8 16.1 %collective-permute-start.9 = (bf16[8,256,128]{2,1,0:T(8,128)(2,1)S(1)}, bf16[8,256,128]{2,1,0:T(8,128)(2,1)}, u32[]{:S(2)}, u32[]{:S(2)}) collective-permute-start(bf16[8,256,128]{2,1,0:T(8,128)(2,1)S(1)} %all_to_all.26.refs_0_), channel_id=1, source_target_pairs={{0,48},{16,0},{32,16},{48,32},{1,49},{17,1},{33,17},{49,33},{2,50}... | collective-permute-start | bytes 1572872 | tf_op jit(solution)/shard_map/ppermute | solution.py:355
  129.5 25.3 %collective-permute-start.7 = (bf16[8,256,128]{2,1,0:T(8,128)(2,1)S(1)}, bf16[8,256,128]{2,1,0:T(8,128)(2,1)}, u32[]{:S(2)}, u32[]{:S(2)}) collective-permute-start(bf16[8,256,128]{2,1,0:T(8,128)(2,1)S(1)} %all_to_all.26.refs_0_), channel_id=1, source_target_pairs={{0,32},{16,48},{32,0},{48,16},{1,33},{17,49},{33,1},{49,17},{2,34}... | collective-permute-start | bytes 1572872 | tf_op jit(solution)/shard_map/ppermute | solution.py:355
  132.3 25.8 %collective-permute-start.5 = (bf16[8,256,128]{2,1,0:T(8,128)(2,1)S(1)}, bf16[8,256,128]{2,1,0:T(8,128)(2,1)}, u32[]{:S(2)}, u32[]{:S(2)}) collective-permute-start(bf16[8,256,128]{2,1,0:T(8,128)(2,1)S(1)} %all_to_all.26.refs_0_), channel_id=1, source_target_pairs={{0,16},{16,32},{32,48},{48,0},{1,17},{17,33},{33,49},{49,1},{2,18}... | collective-permute-start | bytes 1572872 | tf_op jit(solution)/shard_map/ppermute | solution.py:355
  134.3 44.2 %collective-permute-start.4 = (bf16[8,256,128]{2,1,0:T(8,128)(2,1)S(1)}, bf16[8,256,128]{2,1,0:T(8,128)(2,1)S(1)}, u32[]{:S(2)}, u32[]{:S(2)}) collective-permute-start(bf16[8,256,128]{2,1,0:T(8,128)(2,1)S(1)} %all_to_all.26.refs_0_), channel_id=1, source_target_pairs={{0,1},{1,0},{2,3},{3,2},{4,5},{5,4},{6,7},{7,6},{8,9},{9,8},{10,11... | collective-permute-start | bytes 1572872 | tf_op jit(solution)/shard_map/ppermute | solution.py:358
  139.9 38.6 %collective-permute-start.10 = (bf16[8,256,128]{2,1,0:T(8,128)(2,1)}, bf16[8,256,128]{2,1,0:T(8,128)(2,1)S(1)}, u32[]{:S(2)}, u32[]{:S(2)}) collective-permute-start(bf16[8,256,128]{2,1,0:T(8,128)(2,1)} %collective-permute-done.9.refs_3_), channel_id=1, source_target_pairs={{0,1},{1,0},{2,3},{3,2},{4,5},{5,4},{6,7},{7,6},{8,9},{9,8},{10,11... | collective-permute-start | bytes 1572872 | tf_op jit(solution)/shard_map/ppermute | solution.py:358
  154.8 23.7 %collective-permute-start.8 = (bf16[8,256,128]{2,1,0:T(8,128)(2,1)}, bf16[8,256,128]{2,1,0:T(8,128)(2,1)S(1)}, u32[]{:S(2)}, u32[]{:S(2)}) collective-permute-start(bf16[8,256,128]{2,1,0:T(8,128)(2,1)} %collective-permute-done.7.refs_2_), channel_id=1, source_target_pairs={{0,1},{1,0},{2,3},{3,2},{4,5},{5,4},{6,7},{7,6},{8,9},{9,8},{10,11... | collective-permute-start | bytes 1572872 | tf_op jit(solution)/shard_map/ppermute | solution.py:358
  158.1 20.4 %collective-permute-start.6 = (bf16[8,256,128]{2,1,0:T(8,128)(2,1)}, bf16[8,256,128]{2,1,0:T(8,128)(2,1)}, u32[]{:S(2)}, u32[]{:S(2)}) collective-permute-start(bf16[8,256,128]{2,1,0:T(8,128)(2,1)} %collective-permute-done.5.refs_1_), channel_id=1, source_target_pairs={{0,1},{1,0},{2,3},{3,2},{4,5},{5,4},{6,7},{7,6},{8,9},{9,8},{10,11... | collective-permute-start | bytes 1572872 | tf_op jit(solution)/shard_map/ppermute | solution.py:358
  160.5 18.0 %all-to-all-start.3 = ((bf16[64,8,256]{2,1,0:T(8,128)(2,1)}), bf16[64,8,256]{2,1,0:T(8,128)(2,1)S(1)}, u32[]{:S(2)}, u32[]{:S(2)}) async-start(bf16[64,8,256]{2,1,0:T(8,128)(2,1)} %get-tuple-element.21), calls=%async_computation.3 | async-start | bytes 524288 | tf_op jit(solution)/shard_map/all_to_all | solution.py:360
where the time goes:
time: 209 us; the launch traced here: 208 us
  blocking collectives  67.4 us (32%)
  starting transfers between devices  65.3 us (31%)
  Pallas kernels  37.4 us (18%)
  waiting for transfers between devices  33.9 us (16%)
  local copies, waits for them, and re-layouts  2.17 us (1%)
    pallas_call x12, Pallas kernels, call(): pl.pallas_call(kernel, in_specs=[spec(a) for a in args], out_specs=jax.tr...  37.4 us
    all_to_all x1, blocking collectives, layer(): mine = lax.all_to_all(x_sum(near, other, parts), 'z', 0, 0)  27.8 us
    ppermute x4, starting transfers between devices, swapped(): return lax.ppermute(pieces[k], 'core', swap)  24.8 us
    all_to_all x1, blocking collectives, layer(): return (out_feats, *final(lax.all_to_all(back, 'rep', 0, 0), base))  21.8 us
    ppermute x3, waiting for transfers between devices, layer(): lax.ppermute(core_sum(near, other, k), 'x', shift(NX, k))  19.3 us
    all_to_all x1, blocking collectives, layer(): column = lax.all_to_all(d_sum, 'z', 0, 0)  17.8 us
    ppermute x3, starting transfers between devices, layer(): lax.ppermute(core_sum(near, other, k), 'x', shift(NX, k))  11.6 us
    ppermute x3, starting transfers between devices, shifted(): return lax.ppermute(column, 'x', shift(NX, k))  10.4 us
  transfers between devices with their start and end apart: 13, of which 6 were waited for; matrix products, arithmetic and copies ran while one was open for 0% of the time, Pallas kernels for 9%

commit v1 on v0

--- a/solution.py
+++ b/solution.py
@@ -14,6 +14,7 @@
 H = 256
 TILES = 128
 SLOTS = 144
+UNROLL = 8
 HALF = NX * NZ
 DEG = 8
 GRAD = 8
@@ -76,7 +77,7 @@
     return call(spread_kernel, pltpu.VMEM((NR, H, T), BF), feats)
 
 
-def order_kernel(owners, sources, meta, ids, owner_slots, srcs, pairs, seen):
+def order_kernel(owners, sources, meta, ids, owner_slots, srcs, steps_of, seen):
     count, my_core = meta[0], meta[2]
 
     def bucket(t):
@@ -99,10 +100,16 @@
 
             @pl.when(size % 2 == 1)
             def _():
-                ids[at], owner_slots[at], srcs[at] = -1, 0, src
+                ids[at], owner_slots[at], srcs[at] = TILES, 0, src
 
             at = at + size % 2
-        pairs[far] = (at - far * SLOTS) // 2
+        size = at - far * SLOTS
+        steps = (size + 2 * UNROLL - 1) // (2 * UNROLL)
+        steps_of[far] = steps
+
+        @pl.loop(size, steps * 2 * UNROLL)
+        def _(k):
+            ids[far * SLOTS + k], owner_slots[far * SLOTS + k], srcs[far * SLOTS + k] = TILES, 0, 0
 
     @pl.loop(0, count)
     def _(t):
@@ -120,65 +127,51 @@
     return call(order_kernel, out_shape, owners, sources, meta, scratch=scratch)
 
 
-def over_pairs(far, ids, pairs, vals, buffers, prepare, step):
-    tiles, sems = buffers
-    first, n_pairs = far * SLOTS, pairs[far]
-
-    def copy(k):
-        return pltpu.make_async_copy(vals.at[ids[first + k]], tiles.at[k], sems.at[k])
-
-    @pl.loop(0, n_pairs * 2)
-    def _(k):
-        real = ids[first + k] >= 0
-
-        @pl.when(real)
-        def _():
-            copy(k).start()
-
-        @pl.when(jnp.logical_not(real))
-        def _():
-            tiles[k] = jnp.zeros((T, T), BF)
-
+def with_tiles(vals, tiles, sems, prepare):
+    part = TILES // sems.shape[0]
+    copies = [
+        pltpu.make_async_copy(vals.at[pl.ds(k * part, part)], tiles.at[pl.ds(k * part, part)], sems.at[k])
+        for k in range(TILES // part)
+    ]
+    for copy in copies:
+        copy.start()
+    tiles[TILES] = jnp.zeros((T, T), BF)
     prepare()
-
-    def run(ps):
-        for p in ps:
-            copy(p * 2).wait()
-
-            @pl.when(ids[first + p * 2 + 1] >= 0)
-            def _():
-                copy(p * 2 + 1).wait()
-
-        step([(first + p * 2, tiles[pl.ds(p * 2, 2)].reshape(2 * T, T)) for p in ps])
-
-    @pl.loop(0, n_pairs // 2)
+    for copy in copies:
+        copy.wait()
+
+
+def over_pairs(far, ids, steps_of, tiles, step):
+    @pl.loop(0, steps_of[far])
     def _(q):
-        run([q * 2, q * 2 + 1])
-
-    @pl.when(n_pairs % 2 == 1)
-    def _():
-        run([n_pairs - 1])
-
-
-def forward_sums(far, ids, slots, srcs, pairs, my_x, vals, panel, acc, lhs, buffers):
-    def prepare():
-        acc[...] = jnp.zeros(acc.shape, F32)
-        for s in range(NR):
-            lhs[s, :H] = panel[s]
-            lhs[s, H:] = jnp.ones((2 * DEG, T), BF)
-
-    def step(tiles):
-        prods = [dot(lhs[srcs[n]], pair, NT) for n, pair in tiles]
-        for (n, _), prod in zip(tiles, prods):
+        ns = [far * SLOTS + (q * UNROLL + k) * 2 for k in range(UNROLL)]
+        step([(n, jnp.concatenate([tiles[ids[n]], tiles[ids[n + 1]]], axis=0)) for n in ns])
+
+
+def forward_prepare(panel, acc, lhs):
+    acc[...] = jnp.zeros(acc.shape, F32)
+    for s in range(NR):
+        lhs[s, :H] = panel[s]
+        lhs[s, H:] = jnp.ones((2 * DEG, T), BF)
+
+
+def forward_sums(far, lists, tiles, acc, lhs):
+    ids, slots, srcs, steps_of, my_x = lists
+
+    def step(pairs):
+        prods = [dot(lhs[srcs[n]], pair, NT) for n, pair in pairs]
+        for (n, _), prod in zip(pairs, prods):
             for k in range(2):
                 slot = (slots[n + k] - my_x[0] * NZ) & (HALF - 1)
                 acc[slot] = acc[slot] + prod[: H + DEG, k * T : (k + 1) * T]
 
-    over_pairs(far, ids, pairs, vals, buffers, prepare, step)
-
-
-def forward_far_kernel(ids, slots, srcs, pairs, my_x, vals, panel, out, acc, lhs, *buffers):
-    forward_sums(1, ids, slots, srcs, pairs, my_x, vals, panel, acc, lhs, buffers)
+    over_pairs(far, ids, steps_of, tiles, step)
+
+
+def forward_far_kernel(*refs):
+    *lists, vals, panel, out, tiles, acc, lhs, sems = refs
+    with_tiles(vals, tiles, sems, lambda: forward_prepare(panel, acc, lhs))
+    forward_sums(1, lists, tiles, acc, lhs)
 
     @pl.loop(0, HALF)
     def _(b):
@@ -186,25 +179,27 @@
         out[b, H:] = split_degree(acc[b, H:])
 
 
-def forward_near_kernel(ids, slots, srcs, pairs, my_x, vals, panel, out, lhs, *buffers):
-    forward_sums(0, ids, slots, srcs, pairs, my_x, vals, panel, out, lhs, buffers)
-
-
-FORWARD_COST = pl.CostEstimate(flops=64 * 2 * BLK * T * T, bytes_accessed=2**21, transcendentals=0)
-BACKWARD_COST = FORWARD_COST
-BUFFERS = [pltpu.VMEM((SLOTS, T, T), BF), pltpu.SemaphoreType.DMA((SLOTS,))]
-
-
-def forward_far(lists, my_x, tiles, panel):
-    scratch = [pltpu.VMEM((HALF, H + DEG, T), F32), pltpu.VMEM((NR, BLK, T), BF), *BUFFERS]
-    out_shape = pltpu.VMEM((HALF, BLK, T), BF)
-    return call(forward_far_kernel, out_shape, *lists, my_x, tiles, panel, scratch=scratch, cost=FORWARD_COST)
-
-
-def forward_near(lists, my_x, tiles, panel):
-    scratch = [pltpu.VMEM((NR, BLK, T), BF), *BUFFERS]
+def forward_near_kernel(*refs):
+    *lists, tiles, panel, out, lhs = refs
+    forward_prepare(panel, out, lhs)
+    forward_sums(0, lists, tiles, out, lhs)
+
+
+COST = pl.CostEstimate(flops=64 * 2 * BLK * T * T, bytes_accessed=2**21, transcendentals=0)
+LOADED = pltpu.VMEM((TILES + 1, T, T), BF)
+SEMS = pltpu.SemaphoreType.DMA((4,))
+
+
+def forward_far(lists, vals, panel):
+    scratch = [pltpu.VMEM((HALF, H + DEG, T), F32), pltpu.VMEM((NR, BLK, T), BF), SEMS]
+    out_shape = (pltpu.VMEM((HALF, BLK, T), BF), LOADED)
+    return call(forward_far_kernel, out_shape, *lists, vals, panel, scratch=scratch, cost=COST)
+
+
+def forward_near(lists, tiles, panel):
+    scratch = [pltpu.VMEM((NR, BLK, T), BF)]
     out_shape = pltpu.VMEM((HALF, H + DEG, T), F32)
-    return call(forward_near_kernel, out_shape, *lists, my_x, tiles, panel, scratch=scratch, cost=FORWARD_COST)
+    return call(forward_near_kernel, out_shape, *lists, tiles, panel, scratch=scratch, cost=COST)
 
 
 def core_sum(near, other, dx):
@@ -262,35 +257,38 @@
     return call(node_kernel, out_shape, parts, feats, d_out, w_self, w_neigh, scratch=scratch)
 
 
-def backward_sums(far, ids, slots, srcs, pairs, my_x, vals, pieces, start, acc, lhs, buffers):
-    def prepare():
-        acc[...] = start()
-        for k in range(NX):
-            lhs[k * NZ : (k + 1) * NZ] = pieces[k][...]
+def backward_prepare(pieces, start, acc, lhs):
+    acc[...] = start
+    for k in range(NX):
+        lhs[k * NZ : (k + 1) * NZ] = pieces[k][...]
+
+
+def backward_sums(far, lists, tiles, acc, lhs):
+    ids, slots, srcs, steps_of, my_x = lists
 
     def block(n):
         back = my_x[0] - (slots[n] >> 3)
         return lhs[(back & (NX - 1)) * NZ + (slots[n] & (NZ - 1))]
 
-    def step(tiles):
-        sides = [jnp.concatenate([block(n), block(n + 1)], axis=1) for n, _ in tiles]
-        prods = [dot(side, pair) for side, (_, pair) in zip(sides, tiles)]
-        for (n, _), prod in zip(tiles, prods):
+    def step(pairs):
+        sides = [jnp.concatenate([block(n), block(n + 1)], axis=1) for n, _ in pairs]
+        prods = [dot(side, pair) for side, (_, pair) in zip(sides, pairs)]
+        for (n, _), prod in zip(pairs, prods):
             acc[srcs[n]] = acc[srcs[n]] + prod
 
-    over_pairs(far, ids, pairs, vals, buffers, prepare, step)
-
-
-def backward_near_kernel(ids, slots, srcs, pairs, my_x, vals, *refs):
-    *pieces, out, lhs, tiles, sems = refs
-    zeros = lambda: jnp.zeros(out.shape, F32)
-    backward_sums(0, ids, slots, srcs, pairs, my_x, vals, pieces, zeros, out, lhs, (tiles, sems))
-
-
-def backward_far_kernel(ids, slots, srcs, pairs, my_x, vals, *refs):
-    *pieces, near, grads, out, acc, lhs, tiles, sems = refs
-    start = lambda: near[...]
-    backward_sums(1, ids, slots, srcs, pairs, my_x, vals, pieces, start, acc, lhs, (tiles, sems))
+    over_pairs(far, ids, steps_of, tiles, step)
+
+
+def backward_near_kernel(*refs):
+    lists, vals, pieces, (out, tiles, lhs, sems) = refs[:5], refs[5], refs[6 : 6 + NX], refs[6 + NX :]
+    with_tiles(vals, tiles, sems, lambda: backward_prepare(pieces, jnp.zeros(out.shape, F32), out, lhs))
+    backward_sums(0, lists, tiles, out, lhs)
+
+
+def backward_far_kernel(*refs):
+    lists, tiles, pieces, (near, grads, out, acc, lhs) = refs[:5], refs[5], refs[6 : 6 + NX], refs[6 + NX :]
+    backward_prepare(pieces, near[...], acc, lhs)
+    backward_sums(1, lists, tiles, acc, lhs)
     grad = jnp.sum(grads[...].astype(F32), axis=0)
     high = grad.astype(BF).astype(F32)
     parts = [p[:, k : k + T] for p in (high, grad - high) for k in range(0, H, T)]
@@ -300,18 +298,17 @@
         out[s, H:] = grad_rows
 
 
-def backward_near(lists, my_x, tiles, pieces):
-    scratch = [pltpu.VMEM((HALF, H, T), BF), *BUFFERS]
-    out_shape = pltpu.VMEM((NR, H, T), F32)
-    args = (*lists, my_x, tiles, *pieces)
-    return call(backward_near_kernel, out_shape, *args, scratch=scratch, cost=BACKWARD_COST)
-
-
-def backward_far(lists, my_x, tiles, pieces, near, grads):
-    scratch = [pltpu.VMEM((NR, H, T), F32), pltpu.VMEM((HALF, H, T), BF), *BUFFERS]
+def backward_near(lists, vals, pieces):
+    scratch = [pltpu.VMEM((HALF, H, T), BF), SEMS]
+    out_shape = (pltpu.VMEM((NR, H, T), F32), LOADED)
+    return call(backward_near_kernel, out_shape, *lists, vals, *pieces, scratch=scratch, cost=COST)
+
+
+def backward_far(lists, tiles, pieces, near, grads):
+    scratch = [pltpu.VMEM((NR, H, T), F32), pltpu.VMEM((HALF, H, T), BF)]
     out_shape = pltpu.VMEM((NR, H + 4 * GRAD, T), BF)
-    args = (*lists, my_x, tiles, *pieces, near, grads)
-    return call(backward_far_kernel, out_shape, *args, scratch=scratch, cost=BACKWARD_COST)
+    args = (*lists, tiles, *pieces, near, grads)
+    return call(backward_far_kernel, out_shape, *args, scratch=scratch, cost=COST)
 
 
 def final_kernel(parts, base, out, *grads):
@@ -342,9 +339,9 @@
     swap = shift(NC, 1)
 
     panel = lax.all_to_all(spread(feats), "rep", 0, 0)
-    lists = order(tile_owner[0, 0], tile_src[0, 0], meta)
-    far = forward_far(lists, my_x, tiles, panel)
-    near = forward_near(lists, my_x, tiles, panel)
+    lists = (*order(tile_owner[0, 0], tile_src[0, 0], meta), my_x)
+    far, loaded = forward_far(lists, tiles, panel)
+    near = forward_near(lists, loaded, panel)
     other = lax.ppermute(far, "core", swap)
     parts = [lax.ppermute(core_sum(near, other, k), "x", shift(NX, k)) for k in range(1, NX)]
     mine = lax.all_to_all(x_sum(near, other, parts), "z", 0, 0)
@@ -361,8 +358,8 @@
     column = lax.all_to_all(d_sum, "z", 0, 0)
     pieces = [column] + [shifted(k) for k in range(1, NX)]
     others = [swapped(k) for k in range(NX)]
-    back = backward_near(lists, my_x, tiles, pieces)
-    back = backward_far(lists, my_x, tiles, others, back, grads)
+    back, loaded = backward_near(lists, tiles, pieces)
+    back = backward_far(lists, loaded, others, back, grads)
     return (out_feats, *final(lax.all_to_all(back, "rep", 0, 0), base))
 
 

time: 209 us -> 201 us (0.962)
  Pallas kernels: 37.4 us -> 25.1 us
  local copies, waits for them, and re-layouts: 2.17 us -> 6.32 us
    pallas_call x12, Pallas kernels: 37.4 us -> 25.1 us  [call(): pl.pallas_call(kernel, in_specs=[spec(a) for a in args], out_specs=jax.tr...]
    unnamed x14 -> x18, local copies, waits for them, and re-layouts: 2.17 us -> 6.32 us
  transfers between devices with their start and end apart: 13 -> 13, of which waited for: 6 -> 7; matrix products, arithmetic and copies ran while one was open for 0% -> 0% of each run, Pallas kernels for 9% -> 6%
where the time goes in v1:
time: 201 us; the launch traced here: 200 us
  starting transfers between devices  66.1 us (33%)
  blocking collectives  65.7 us (33%)
  waiting for transfers between devices  35.1 us (17%)
  Pallas kernels  25.1 us (12%)
  local copies, waits for them, and re-layouts  6.32 us (3%)
    all_to_all x1, blocking collectives, layer(): mine = lax.all_to_all(x_sum(near, other, parts), 'z', 0, 0)  26.5 us
    pallas_call x12, Pallas kernels, call(): pl.pallas_call(kernel, in_specs=[spec(a) for a in args], out_specs=jax.tr...  25.1 us
    ppermute x4, starting transfers between devices, swapped(): return lax.ppermute(pieces[k], 'core', swap)  24.9 us
    all_to_all x1, blocking collectives, layer(): return (out_feats, *final(lax.all_to_all(back, 'rep', 0, 0), base))  21.8 us
    ppermute x3, waiting for transfers between devices, layer(): lax.ppermute(core_sum(near, other, k), 'x', shift(NX, k))  19.7 us
    all_to_all x1, blocking collectives, layer(): column = lax.all_to_all(d_sum, 'z', 0, 0)  17.4 us
    ppermute x3, starting transfers between devices, layer(): lax.ppermute(core_sum(near, other, k), 'x', shift(NX, k))  11.8 us
    ppermute x3, starting transfers between devices, shifted(): return lax.ppermute(column, 'x', shift(NX, k))  10.7 us
  transfers between devices with their start and end apart: 13, of which 7 were waited for; matrix products, arithmetic and copies ran while one was open for 0% of the time, Pallas kernels for 6%

profile of v1, /device:TPU:1, one launch (start us, length us, event | category | flops | bytes accessed | tf_op | source)
XLA Modules:
  0.0 199.9 jit_solution(3565461968135725969)
XLA Ops:
  0.6 0.0 copy-start.2
  0.6 0.8 copy-done.2
  1.5 0.9 shard_map.112
  2.4 7.6 %all-to-all-start = ((bf16[8,256,128]{2,1,0:T(8,128)(2,1)}), bf16[8,256,128]{2,1,0:T(8,128)(2,1)S(1)}, u32[]{:S(2)}, u32[]{:S(2)}) async-start(bf16[8,256,128]{2,1,0:T(8,128)(2,1)} %shard_map.112), calls=%async_computation | async-start | bytes 1048576 | tf_op jit(solution)/shard_map/all_to_all | solution.py:341
  10.7 0.1 pad_add_fusion.meta
  10.8 0.0 copy-start.7
  10.8 0.7 copy-done.7
  11.4 0.0 copy-start.8
  11.4 0.7 copy-done.8
  12.1 4.2 %shard_map.111 = (s32[288]{0:T(512)S(1)}, s32[288]{0:T(512)S(1)}, s32[288]{0:T(512)S(1)}, s32[2]{0:T(128)S(1)}) custom-call(s32[128]{0:T(128)S(1)} %bitcast.7, s32[128]{0:T(128)S(1)} %bitcast.8, s32[3]{0:T(128)S(1)} %pad_add_fusion.meta), custom_call_target="tpu_custom_call" | custom-call | tf_op jit(solution)/shard_map/pallas_call | solution.py:43
  16.3 8.7 %all-to-all-done.refs_6_ = bf16[8,256,128]{2,1,0:T(8,128)(2,1)S(1)} async-done(((bf16[8,256,128]{2,1,0:T(8,128)(2,1)}), bf16[8,256,128]{2,1,0:T(8,128)(2,1)S(1)}, u32[]{:S(2)}, u32[]{:S(2)}) %all-to-all-start) | async-done | bytes 524320 | tf_op jit(solution)/shard_map/all_to_all | solution.py:341
  25.0 5.5 %shard_map.113 = (bf16[32,272,128]{2,1,0:T(8,128)(2,1)S(1)}, bf16[129,128,128]{2,1,0:T(8,128)(2,1)S(1)}) custom-call(s32[288]{0:T(512)S(1)} %get-tuple-element.19.refs_0_, s32[288]{0:T(512)S(1)} %get-tuple-element.20.refs_1_, s32[288]{0:T(512)S(1)} %get-tuple-element.21.refs_2_, s32[2]{0:T(128)S(1)} %get-tuple-element.22.refs_3_, s32[1]{0:T(128)} %bitcast.3.refs_4_, ...), custom_call_target="tpu_custom_call" | custom-call | flops 570425344 | bytes 2097152 | tf_op jit(solution)/shard_map/pallas_call | solution.py:43
  30.5 4.8 %collective-permute-start = (bf16[32,272,128]{2,1,0:T(8,128)(2,1)S(1)}, bf16[32,272,128]{2,1,0:T(8,128)(2,1)S(1)}, u32[]{:S(2)}, u32[]{:S(2)}) collective-permute-start(bf16[32,272,128]{2,1,0:T(8,128)(2,1)S(1)} %get-tuple-element.24), channel_id=1, source_target_pairs={{0,1},{1,0},{2,3},{3,2},{4,5},{5,4},{6,7},{7,6},{8,9},{9,8},{10,11... | collective-permute-start | bytes 6684680 | tf_op jit(solution)/shard_map/ppermute | solution.py:345
  35.3 3.0 %shard_map.114.a.near = f32[32,264,128]{2,1,0:T(8,128)S(1)} custom-call(s32[288]{0:T(512)S(1)} %get-tuple-element.19.refs_0_, s32[288]{0:T(512)S(1)} %get-tuple-element.20.refs_1_, s32[288]{0:T(512)S(1)} %get-tuple-element.21.refs_2_, s32[2]{0:T(128)S(1)} %get-tuple-element.22.refs_3_, s32[1]{0:T(128)} %bitcast.3.refs_4_, ...), custom_call_target="tpu_custom_call" | custom-call | flops 570425344 | bytes 2097152 | tf_op jit(solution)/shard_map/pallas_call | solution.py:43
  38.4 0.9 collective-permute-done.b.other
  39.3 0.2 shard_map.115
  39.4 4.2 %collective-permute-start.1 = (bf16[8,272,128]{2,1,0:T(8,128)(2,1)S(1)}, bf16[8,272,128]{2,1,0:T(8,128)(2,1)S(1)}, u32[]{:S(2)}, u32[]{:S(2)}) collective-permute-start(bf16[8,272,128]{2,1,0:T(8,128)(2,1)S(1)} %shard_map.115), channel_id=1, source_target_pairs={{0,16},{16,32},{32,48},{48,0},{1,17},{17,33},{33,49},{49,1},{2,18}... | collective-permute-start | bytes 1671176 | tf_op jit(solution)/shard_map/ppermute | solution.py:346
  43.7 0.2 shard_map.116
  43.8 3.8 %collective-permute-start.2 = (bf16[8,272,128]{2,1,0:T(8,128)(2,1)S(1)}, bf16[8,272,128]{2,1,0:T(8,128)(2,1)S(1)}, u32[]{:S(2)}, u32[]{:S(2)}) collective-permute-start(bf16[8,272,128]{2,1,0:T(8,128)(2,1)S(1)} %shard_map.116), channel_id=1, source_target_pairs={{0,32},{16,48},{32,0},{48,16},{1,33},{17,49},{33,1},{49,17},{2,34}... | collective-permute-start | bytes 1671176 | tf_op jit(solution)/shard_map/ppermute | solution.py:346
  47.7 0.2 shard_map.117
  47.8 0.0 copy-start.3
  47.8 0.0 copy-start.4
  47.8 0.0 copy-start.5
  47.9 0.0 copy-start.6
  47.9 3.8 %collective-permute-start.3 = (bf16[8,272,128]{2,1,0:T(8,128)(2,1)S(1)}, bf16[8,272,128]{2,1,0:T(8,128)(2,1)S(1)}, u32[]{:S(2)}, u32[]{:S(2)}) collective-permute-start(bf16[8,272,128]{2,1,0:T(8,128)(2,1)S(1)} %shard_map.117), channel_id=1, source_target_pairs={{0,48},{16,0},{32,16},{48,32},{1,49},{17,1},{33,17},{49,33},{2,50}... | collective-permute-start | bytes 1671176 | tf_op jit(solution)/shard_map/ppermute | solution.py:346
  51.6 5.4 %collective-permute-done.1.refs_0_ = bf16[8,272,128]{2,1,0:T(8,128)(2,1)S(1)} collective-permute-done((bf16[8,272,128]{2,1,0:T(8,128)(2,1)S(1)}, bf16[8,272,128]{2,1,0:T(8,128)(2,1)S(1)}, u32[]{:S(2)}, u32[]{:S(2)}) %collective-permute-start.1) | collective-permute-done | bytes 557088 | tf_op jit(solution)/shard_map/ppermute | solution.py:346
  57.0 12.8 %collective-permute-done.2.refs_1_ = bf16[8,272,128]{2,1,0:T(8,128)(2,1)S(1)} collective-permute-done((bf16[8,272,128]{2,1,0:T(8,128)(2,1)S(1)}, bf16[8,272,128]{2,1,0:T(8,128)(2,1)S(1)}, u32[]{:S(2)}, u32[]{:S(2)}) %collective-permute-start.2) | collective-permute-done | bytes 557088 | tf_op jit(solution)/shard_map/ppermute | solution.py:346
  69.8 1.5 collective-permute-done.3.refs_2_
  71.4 0.4 shard_map.118
  71.8 26.5 %all_to_all.25.parts = bf16[8,272,128]{2,1,0:T(8,128)(2,1)S(1)} all-to-all(bf16[8,272,128]{2,1,0:T(8,128)(2,1)S(1)} %shard_map.118), channel_id=1, replica_groups=mesh['rep'=8,'x'=4,'z'=8,'core'=2] {'z'}, dimensions={0} | all-to-all | bytes 1114112 | tf_op jit(solution)/shard_map/all_to_all | solution.py:347
  98.2 0.0 copy-done.3
  98.2 0.0 copy-done.4
  98.2 0.0 copy-done.5
  98.2 0.0 copy-done.6
  98.3 1.3 shard_map.119
  99.6 17.4 %all_to_all.26.refs_6_ = bf16[8,256,128]{2,1,0:T(8,128)(2,1)S(1)} all-to-all(bf16[8,256,128]{2,1,0:T(8,128)(2,1)S(1)} %get-tuple-element.26), channel_id=1, replica_groups=mesh['rep'=8,'x'=4,'z'=8,'core'=2] {'z'}, dimensions={0} | all-to-all | bytes 1048576 | tf_op jit(solution)/shard_map/all_to_all | solution.py:358
  117.0 5.8 %collective-permute-start.6 = (bf16[8,256,128]{2,1,0:T(8,128)(2,1)S(1)}, bf16[8,256,128]{2,1,0:T(8,128)(2,1)}, u32[]{:S(2)}, u32[]{:S(2)}) collective-permute-start(bf16[8,256,128]{2,1,0:T(8,128)(2,1)S(1)} %all_to_all.26.refs_6_), channel_id=1, source_target_pairs={{0,48},{16,0},{32,16},{48,32},{1,49},{17,1},{33,17},{49,33},{2,50}... | collective-permute-start | bytes 1572872 | tf_op jit(solution)/shard_map/ppermute | solution.py:352
  122.8 3.0 %collective-permute-start.5 = (bf16[8,256,128]{2,1,0:T(8,128)(2,1)S(1)}, bf16[8,256,128]{2,1,0:T(8,128)(2,1)}, u32[]{:S(2)}, u32[]{:S(2)}) collective-permute-start(bf16[8,256,128]{2,1,0:T(8,128)(2,1)S(1)} %all_to_all.26.refs_6_), channel_id=1, source_target_pairs={{0,32},{16,48},{32,0},{48,16},{1,33},{17,49},{33,1},{49,17},{2,34}... | collective-permute-start | bytes 1572872 | tf_op jit(solution)/shard_map/ppermute | solution.py:352
  125.8 1.9 collective-permute-start.4
  127.8 6.2 %collective-permute-start.7 = (bf16[8,256,128]{2,1,0:T(8,128)(2,1)S(1)}, bf16[8,256,128]{2,1,0:T(8,128)(2,1)S(1)}, u32[]{:S(2)}, u32[]{:S(2)}) collective-permute-start(bf16[8,256,128]{2,1,0:T(8,128)(2,1)S(1)} %all_to_all.26.refs_6_), channel_id=1, source_target_pairs={{0,1},{1,0},{2,3},{3,2},{4,5},{5,4},{6,7},{7,6},{8,9},{9,8},{10,11... | collective-permute-start | bytes 1572872 | tf_op jit(solution)/shard_map/ppermute | solution.py:355
  134.0 0.0 collective-permute-done.6.refs_9_
  134.0 14.1 %collective-permute-start.10 = (bf16[8,256,128]{2,1,0:T(8,128)(2,1)}, bf16[8,256,128]{2,1,0:T(8,128)(2,1)S(1)}, u32[]{:S(2)}, u32[]{:S(2)}) collective-permute-start(bf16[8,256,128]{2,1,0:T(8,128)(2,1)} %collective-permute-done.6.refs_9_), channel_id=1, source_target_pairs={{0,1},{1,0},{2,3},{3,2},{4,5},{5,4},{6,7},{7,6},{8,9},{9,8},{10,11... | collective-permute-start | bytes 1572872 | tf_op jit(solution)/shard_map/ppermute | solution.py:355
  148.1 0.0 collective-permute-done.5.refs_8_
  148.1 1.9 collective-permute-start.9
  150.0 1.1 collective-permute-done.4.refs_7_
  151.1 2.7 %collective-permute-start.8 = (bf16[8,256,128]{2,1,0:T(8,128)(2,1)}, bf16[8,256,128]{2,1,0:T(8,128)(2,1)}, u32[]{:S(2)}, u32[]{:S(2)}) collective-permute-start(bf16[8,256,128]{2,1,0:T(8,128)(2,1)} %collective-permute-done.4.refs_7_), channel_id=1, source_target_pairs={{0,1},{1,0},{2,3},{3,2},{4,5},{5,4},{6,7},{7,6},{8,9},{9,8},{10,11... | collective-permute-start | bytes 1572872 | tf_op jit(solution)/shard_map/ppermute | solution.py:355
  153.8 6.3 %all-to-all-start.3 = ((bf16[64,8,256]{2,1,0:T(8,128)(2,1)}), bf16[64,8,256]{2,1,0:T(8,128)(2,1)S(1)}, u32[]{:S(2)}, u32[]{:S(2)}) async-start(bf16[64,8,256]{2,1,0:T(8,128)(2,1)} %get-tuple-element.29), calls=%async_computation.3 | async-start | bytes 524288 | tf_op jit(solution)/shard_map/all_to_all | solution.py:357
  160.1 5.4 %shard_map.120 = (f32[8,256,128]{2,1,0:T(8,128)S(1)}, bf16[129,128,128]{2,1,0:T(8,128)(2,1)S(1)}) custom-call(s32[288]{0:T(512)S(1)} %get-tuple-element.19.refs_0_, s32[288]{0:T(512)S(1)} %get-tuple-element.20.refs_1_, s32[288]{0:T(512)S(1)} %get-tuple-element.21.refs_2_, s32[2]{0:T(128)S(1)} %get-tuple-element.22.refs_3_, s32[1]{0:T(128)} %bitcast.3.refs_4_, ...), custom_call_target="tpu_custom_call" | custom-call | flops 570425344 | bytes 2097152 | tf_op jit(solution)/shard_map/pallas_call | solution.py:43
  165.4 0.0 copy-start
  165.4 2.0 copy-done
  167.4 4.6 %all-to-all-done.3.refs_11_ = bf16[64,8,256]{2,1,0:T(8,128)(2,1)S(1)} async-done(((bf16[64,8,256]{2,1,0:T(8,128)(2,1)}), bf16[64,8,256]{2,1,0:T(8,128)(2,1)S(1)}, u32[]{:S(2)}, u32[]{:S(2)}) %all-to-all-start.3) | async-done | bytes 262176 | tf_op jit(solution)/shard_map/all_to_all | solution.py:357
  172.0 0.0 collective-permute-done.7.refs_6_
  172.0 0.0 collective-permute-done.10.refs_9_
  172.0 0.0 collective-permute-done.9.refs_8_
  172.0 0.0 collective-permute-done.8.refs_7_
  172.1 0.0 copy-start.1
  172.1 2.2 %copy-done.1 = bf16[129,128,128]{2,1,0:T(8,128)(2,1)S(1)} copy-done((bf16[129,128,128]{2,1,0:T(8,128)(2,1)S(1)}, bf16[129,128,128]{2,1,0:T(8,128)(2,1)}, u32[]{:S(2)}) %copy-start.1) | copy-done | bytes 4227096
  174.3 3.1 %shard_map.121 = bf16[8,288,128]{2,1,0:T(8,128)(2,1)S(1)} custom-call(s32[288]{0:T(512)S(1)} %get-tuple-element.19.refs_0_, s32[288]{0:T(512)S(1)} %get-tuple-element.20.refs_1_, s32[288]{0:T(512)S(1)} %get-tuple-element.21.refs_2_, s32[2]{0:T(128)S(1)} %get-tuple-element.22.refs_3_, s32[1]{0:T(128)} %bitcast.3.refs_4_, ...), custom_call_target="tpu_custom_call" | custom-call | flops 570425344 | bytes 2097152 | tf_op jit(solution)/shard_map/pallas_call | solution.py:43
  177.4 21.8 %all_to_all.27.parts = bf16[8,288,128]{2,1,0:T(8,128)(2,1)S(1)} all-to-all(bf16[8,288,128]{2,1,0:T(8,128)(2,1)S(1)} %shard_map.121), channel_id=1, replica_groups=mesh['rep'=8,'x'=4,'z'=8,'core'=2] {'rep'}, dimensions={0} | all-to-all | bytes 1179648 | tf_op jit(solution)/shard_map/all_to_all | solution.py:363
  199.2 0.8 shard_map.122
Async XLA Ops:
  0.6 0.8 copy-start.2
  2.4 22.6 %all-to-all-start = ((bf16[8,256,128]{2,1,0:T(8,128)(2,1)}), bf16[8,256,128]{2,1,0:T(8,128)(2,1)S(1)}, u32[]{:S(2)}, u32[]{:S(2)}) async-start(bf16[8,256,128]{2,1,0:T(8,128)(2,1)} %shard_map.112), calls=%async_computation | async-start | bytes 1048576 | tf_op jit(solution)/shard_map/all_to_all | solution.py:341
  10.8 0.7 copy-start.7
  11.4 0.7 copy-start.8
  30.5 8.8 %collective-permute-start = (bf16[32,272,128]{2,1,0:T(8,128)(2,1)S(1)}, bf16[32,272,128]{2,1,0:T(8,128)(2,1)S(1)}, u32[]{:S(2)}, u32[]{:S(2)}) collective-permute-start(bf16[32,272,128]{2,1,0:T(8,128)(2,1)S(1)} %get-tuple-element.24), channel_id=1, source_target_pairs={{0,1},{1,0},{2,3},{3,2},{4,5},{5,4},{6,7},{7,6},{8,9},{9,8},{10,11... | collective-permute-start | bytes 6684680 | tf_op jit(solution)/shard_map/ppermute | solution.py:345
  39.4 17.6 %collective-permute-start.1 = (bf16[8,272,128]{2,1,0:T(8,128)(2,1)S(1)}, bf16[8,272,128]{2,1,0:T(8,128)(2,1)S(1)}, u32[]{:S(2)}, u32[]{:S(2)}) collective-permute-start(bf16[8,272,128]{2,1,0:T(8,128)(2,1)S(1)} %shard_map.115), channel_id=1, source_target_pairs={{0,16},{16,32},{32,48},{48,0},{1,17},{17,33},{33,49},{49,1},{2,18}... | collective-permute-start | bytes 1671176 | tf_op jit(solution)/shard_map/ppermute | solution.py:346
  43.8 26.0 %collective-permute-start.2 = (bf16[8,272,128]{2,1,0:T(8,128)(2,1)S(1)}, bf16[8,272,128]{2,1,0:T(8,128)(2,1)S(1)}, u32[]{:S(2)}, u32[]{:S(2)}) collective-permute-start(bf16[8,272,128]{2,1,0:T(8,128)(2,1)S(1)} %shard_map.116), channel_id=1, source_target_pairs={{0,32},{16,48},{32,0},{48,16},{1,33},{17,49},{33,1},{49,17},{2,34}... | collective-permute-start | bytes 1671176 | tf_op jit(solution)/shard_map/ppermute | solution.py:346
  47.8 50.4 %copy-start.3 = (bf16[128,256]{1,0:T(8,128)(2,1)S(1)}, bf16[128,256]{1,0:T(8,128)(2,1)}, u32[]{:S(2)}) copy-start(bf16[128,256]{1,0:T(8,128)(2,1)} %feats.3) | copy-start | bytes 196612
  47.8 50.4 %copy-start.4 = (bf16[256,256]{1,0:T(8,128)(2,1)S(1)}, bf16[256,256]{1,0:T(8,128)(2,1)}, u32[]{:S(2)}) copy-start(bf16[256,256]{1,0:T(8,128)(2,1)} %w_self.1) | copy-start | bytes 393220
  47.8 50.4 %copy-start.5 = (bf16[256,256]{1,0:T(8,128)(2,1)S(1)}, bf16[256,256]{1,0:T(8,128)(2,1)}, u32[]{:S(2)}) copy-start(bf16[256,256]{1,0:T(8,128)(2,1)} %w_neigh.1) | copy-start | bytes 393220
  47.9 50.4 %copy-start.6 = (bf16[128,256]{1,0:T(8,128)(2,1)S(1)}, bf16[128,256]{1,0:T(8,128)(2,1)}, u32[]{:S(2)}) copy-start(bf16[128,256]{1,0:T(8,128)(2,1)} %d_out.1) | copy-start | bytes 196612
  47.9 23.5 %collective-permute-start.3 = (bf16[8,272,128]{2,1,0:T(8,128)(2,1)S(1)}, bf16[8,272,128]{2,1,0:T(8,128)(2,1)S(1)}, u32[]{:S(2)}, u32[]{:S(2)}) collective-permute-start(bf16[8,272,128]{2,1,0:T(8,128)(2,1)S(1)} %shard_map.117), channel_id=1, source_target_pairs={{0,48},{16,0},{32,16},{48,32},{1,49},{17,1},{33,17},{49,33},{2,50}... | collective-permute-start | bytes 1671176 | tf_op jit(solution)/shard_map/ppermute | solution.py:346
  117.0 16.9 %collective-permute-start.6 = (bf16[8,256,128]{2,1,0:T(8,128)(2,1)S(1)}, bf16[8,256,128]{2,1,0:T(8,128)(2,1)}, u32[]{:S(2)}, u32[]{:S(2)}) collective-permute-start(bf16[8,256,128]{2,1,0:T(8,128)(2,1)S(1)} %all_to_all.26.refs_6_), channel_id=1, source_target_pairs={{0,48},{16,0},{32,16},{48,32},{1,49},{17,1},{33,17},{49,33},{2,50}... | collective-permute-start | bytes 1572872 | tf_op jit(solution)/shard_map/ppermute | solution.py:352
  122.8 25.3 %collective-permute-start.5 = (bf16[8,256,128]{2,1,0:T(8,128)(2,1)S(1)}, bf16[8,256,128]{2,1,0:T(8,128)(2,1)}, u32[]{:S(2)}, u32[]{:S(2)}) collective-permute-start(bf16[8,256,128]{2,1,0:T(8,128)(2,1)S(1)} %all_to_all.26.refs_6_), channel_id=1, source_target_pairs={{0,32},{16,48},{32,0},{48,16},{1,33},{17,49},{33,1},{49,17},{2,34}... | collective-permute-start | bytes 1572872 | tf_op jit(solution)/shard_map/ppermute | solution.py:352
  125.8 25.3 %collective-permute-start.4 = (bf16[8,256,128]{2,1,0:T(8,128)(2,1)S(1)}, bf16[8,256,128]{2,1,0:T(8,128)(2,1)}, u32[]{:S(2)}, u32[]{:S(2)}) collective-permute-start(bf16[8,256,128]{2,1,0:T(8,128)(2,1)S(1)} %all_to_all.26.refs_6_), channel_id=1, source_target_pairs={{0,16},{16,32},{32,48},{48,0},{1,17},{17,33},{33,49},{49,1},{2,18}... | collective-permute-start | bytes 1572872 | tf_op jit(solution)/shard_map/ppermute | solution.py:352
  127.8 44.3 %collective-permute-start.7 = (bf16[8,256,128]{2,1,0:T(8,128)(2,1)S(1)}, bf16[8,256,128]{2,1,0:T(8,128)(2,1)S(1)}, u32[]{:S(2)}, u32[]{:S(2)}) collective-permute-start(bf16[8,256,128]{2,1,0:T(8,128)(2,1)S(1)} %all_to_all.26.refs_6_), channel_id=1, source_target_pairs={{0,1},{1,0},{2,3},{3,2},{4,5},{5,4},{6,7},{7,6},{8,9},{9,8},{10,11... | collective-permute-start | bytes 1572872 | tf_op jit(solution)/shard_map/ppermute | solution.py:355
  134.0 38.1 %collective-permute-start.10 = (bf16[8,256,128]{2,1,0:T(8,128)(2,1)}, bf16[8,256,128]{2,1,0:T(8,128)(2,1)S(1)}, u32[]{:S(2)}, u32[]{:S(2)}) collective-permute-start(bf16[8,256,128]{2,1,0:T(8,128)(2,1)} %collective-permute-done.6.refs_9_), channel_id=1, source_target_pairs={{0,1},{1,0},{2,3},{3,2},{4,5},{5,4},{6,7},{7,6},{8,9},{9,8},{10,11... | collective-permute-start | bytes 1572872 | tf_op jit(solution)/shard_map/ppermute | solution.py:355
  148.1 23.9 %collective-permute-start.9 = (bf16[8,256,128]{2,1,0:T(8,128)(2,1)}, bf16[8,256,128]{2,1,0:T(8,128)(2,1)S(1)}, u32[]{:S(2)}, u32[]{:S(2)}) collective-permute-start(bf16[8,256,128]{2,1,0:T(8,128)(2,1)} %collective-permute-done.5.refs_8_), channel_id=1, source_target_pairs={{0,1},{1,0},{2,3},{3,2},{4,5},{5,4},{6,7},{7,6},{8,9},{9,8},{10,11... | collective-permute-start | bytes 1572872 | tf_op jit(solution)/shard_map/ppermute | solution.py:355
  151.1 20.9 %collective-permute-start.8 = (bf16[8,256,128]{2,1,0:T(8,128)(2,1)}, bf16[8,256,128]{2,1,0:T(8,128)(2,1)}, u32[]{:S(2)}, u32[]{:S(2)}) collective-permute-start(bf16[8,256,128]{2,1,0:T(8,128)(2,1)} %collective-permute-done.4.refs_7_), channel_id=1, source_target_pairs={{0,1},{1,0},{2,3},{3,2},{4,5},{5,4},{6,7},{7,6},{8,9},{9,8},{10,11... | collective-permute-start | bytes 1572872 | tf_op jit(solution)/shard_map/ppermute | solution.py:355
  153.8 18.2 %all-to-all-start.3 = ((bf16[64,8,256]{2,1,0:T(8,128)(2,1)}), bf16[64,8,256]{2,1,0:T(8,128)(2,1)S(1)}, u32[]{:S(2)}, u32[]{:S(2)}) async-start(bf16[64,8,256]{2,1,0:T(8,128)(2,1)} %get-tuple-element.29), calls=%async_computation.3 | async-start | bytes 524288 | tf_op jit(solution)/shard_map/all_to_all | solution.py:357
  165.4 2.0 copy-start
  172.1 2.2 %copy-start.1 = (bf16[129,128,128]{2,1,0:T(8,128)(2,1)S(1)}, bf16[129,128,128]{2,1,0:T(8,128)(2,1)}, u32[]{:S(2)}) copy-start(bf16[129,128,128]{2,1,0:T(8,128)(2,1)} %copy-done) | copy-start | bytes 12681220
